TPU v7x, 32 devices: a whole 2x2x4 slice. The times are simulated.
32 devices in a mesh: head: 4 (over x, core), blk: 8 (over z, y).
Axes of the slice: x: 2, y: 2, z: 4, core: 2. Of those that a mesh axis runs over, the one named last changes fastest.
Arguments:
- layer_input: bfloat16 [4096, 1024], P(('head', 'blk')), may hold values from -6 to 6
- out_grad: bfloat16 [4096, 1024], P(('head', 'blk')), may hold values from -6 to 6
- lengths: int32 [4], replicated, may hold values from 1 to 2048, 3072 in all
- ln_attn: bfloat16 [1024], P(('head', 'blk')), may hold values from 0.5 to 1.5
- w_qkv: bfloat16 [1024, 3072], P(('head', 'blk')), may hold values from -0.1875 to 0.1875
- w_attn_out: bfloat16 [1024, 1024], P(('head', 'blk')), may hold values from -6 to 6
- ln_mlp: bfloat16 [1024], P(('head', 'blk')), may hold values from 0.5 to 1.5
- w_in: bfloat16 [1024, 5248], P(('head', 'blk')), may hold values from -0.1875 to 0.1875
- w_mlp_out: bfloat16 [2624, 1024], P(None, ('head', 'blk')), may hold values from -0.125 to 0.125
Outputs:
- layer_output: float32 [4096, 1024], P(('head', 'blk'))
- input_grad: float32 [4096, 1024], P(('head', 'blk'))
- d_ln_attn: float32 [1024], P(('head', 'blk'))
- d_w_qkv: float32 [1024, 3072], P(('head', 'blk'))
- d_w_attn_out: float32 [1024, 1024], P(('head', 'blk'))
- d_ln_mlp: float32 [1024], P(('head', 'blk'))
- d_w_in: float32 [1024, 5248], P(('head', 'blk'))
- d_w_mlp_out: float32 [2624, 1024], P(None, ('head', 'blk'))
Inputs may be any that keep to these rules, and one draw needn't show every extreme that they name: lengths of the 4 sequences packed from slot 0; they sum to 3072 and the longest is exactly 2048; the remaining slots are padding.
All inputs are finite; a program needn't handle non-finite values.
Results may differ from a plain program's by a relative error of at most 0.023.
Values may be sent and summed in bfloat16 or wider, within the bound.
A program may use at most 192 MiB of HBM per device.

v0:
```python
import jax
import jax.numpy as jnp
from jax import lax
from jax.sharding import PartitionSpec as P

DH = 64
ROPE_BASE = 160000.0
NORM_EPS = 1e-05
MASK_FLOOR = -1e30


def norm_forward(values, gain):
    centre = values - jnp.mean(values, axis=-1, keepdims=True)
    variance = jnp.mean(centre * centre, axis=-1, keepdims=True)
    scale_row = lax.rsqrt(variance + NORM_EPS)
    normed = centre * scale_row
    return (normed * gain, normed, scale_row)


def norm_backward(grad_rows, gain, normed, scale_row):
    scaled_grad = grad_rows * gain
    gain_grad = jnp.sum(grad_rows * normed, axis=0)
    mean_one = jnp.mean(scaled_grad, axis=-1, keepdims=True)
    mean_two = jnp.mean(scaled_grad * normed, axis=-1, keepdims=True)
    return (scale_row * (scaled_grad - mean_one - normed * mean_two), gain_grad)


def locate(rows_at, lengths):
    seq_ends = jnp.cumsum(lengths)
    segment = jnp.sum((rows_at[:, None] >= seq_ends[None, :]).astype(jnp.int32), axis=1)
    seq_starts = jnp.concatenate([seq_ends - lengths, seq_ends[-1:]])
    picked = segment[:, None] == lax.iota(jnp.int32, seq_starts.shape[0])[None, :]
    begins = jnp.sum(jnp.where(picked, seq_starts[None, :], 0), axis=1)
    return (segment, rows_at - begins)


def rotate(values, position, sign_value):
    half_dim = values.shape[-1] // 2
    inv_freq = jnp.power(ROPE_BASE, -2.0 * lax.iota(jnp.float32, half_dim) / values.shape[-1])
    angles = position.astype(jnp.float32)[:, None] * inv_freq[None, :]
    cosine = jnp.cos(angles)[:, None, :]
    sine_part = sign_value * jnp.sin(angles)[:, None, :]
    front_part = values[..., :half_dim]
    back_part = values[..., half_dim:]
    return jnp.concatenate(
        [front_part * cosine - back_part * sine_part, back_part * cosine + front_part * sine_part],
        axis=-1,
    )


def spread(flat_rows, rows_dev, group_rows, cycle_size):
    owner = flat_rows // group_rows
    inner = flat_rows % group_rows
    return inner // rows_dev * (cycle_size * rows_dev) + owner * rows_dev + inner % rows_dev


def block_size(row_count, base_rows):
    for block_rows in (512, base_rows):
        return block_rows
    return row_count


def take_rows(array_in, block_at, block_rows):
    return lax.dynamic_slice_in_dim(array_in, block_at * block_rows, block_rows, 0)


def online(carried, queries, keys_in, values_in, seg_query, seg_key):
    top_score, row_total, weighted = carried
    scores = (
        jnp.einsum("qhd,khd->hqk", queries, keys_in, preferred_element_type=jnp.float32) * 0.125
    )
    same_seq = (seg_query[:, None] == seg_key[None, :])[None]
    scores = jnp.where(same_seq, scores, MASK_FLOOR)
    new_top = jnp.maximum(top_score, jnp.max(scores, axis=-1))
    weights = jnp.where(same_seq, jnp.exp(scores - new_top[:, :, None]), 0.0)
    rescale = jnp.exp(top_score - new_top)
    row_total = row_total * rescale + jnp.sum(weights, axis=-1)
    weighted = weighted * rescale.T[:, :, None] + jnp.einsum(
        "hqk,khd->qhd", weights.astype(jnp.bfloat16), values_in, preferred_element_type=jnp.float32
    )
    return (new_top, row_total, weighted)


def score_grads(query_in, key_in, value_in, grad_rows, lse_in, delta_in, seg_query, seg_key):
    scores = (
        jnp.einsum("qhd,khd->hqk", query_in, key_in, preferred_element_type=jnp.float32) * 0.125
    )
    same_seq = (seg_query[:, None] == seg_key[None, :])[None]
    probs = jnp.exp(jnp.where(same_seq, scores - lse_in[:, :, None], MASK_FLOOR))
    grad_probs = jnp.einsum("qhd,khd->hqk", grad_rows, value_in, preferred_element_type=jnp.float32)
    grad_scores = (probs * (grad_probs - delta_in[:, :, None])).astype(jnp.bfloat16)
    return (probs, grad_scores)


def key_grad_rows(query_in, grad_rows, lse_in, delta_in, seg_query, keys_in, values_in, seg_key):
    probs, grad_scores = score_grads(
        query_in, keys_in, values_in, grad_rows, lse_in, delta_in, seg_query, seg_key
    )
    grad_keys = 0.125 * jnp.einsum(
        "hqk,qhd->khd", grad_scores, query_in, preferred_element_type=jnp.float32
    )
    grad_values = jnp.einsum(
        "hqk,qhd->khd", probs.astype(jnp.bfloat16), grad_rows, preferred_element_type=jnp.float32
    )
    return (grad_keys, grad_values)


def shards(layer_input, out_grad, lengths, ln_attn, w_qkv, w_attn_out, ln_mlp, w_in, w_mlp_out):
    head_groups = lax.axis_size("head")
    cycle_size = lax.axis_size("blk")
    rows_dev = layer_input.shape[0]
    width = layer_input.shape[1]
    all_heads = width // DH
    local_heads = all_heads // head_groups
    local_width = local_heads * DH
    group_rows = head_groups * rows_dev
    nseq_count = lengths.shape[0]
    gain_one, wqkv_full, wout_full, gain_two, win_full, wdown_full = (
        lax.all_gather(ln_attn, ("head", "blk"), axis=0, tiled=True),
        lax.all_gather(w_qkv, ("head", "blk"), axis=0, tiled=True),
        lax.all_gather(w_attn_out, ("head", "blk"), axis=0, tiled=True),
        lax.all_gather(ln_mlp, ("head", "blk"), axis=0, tiled=True),
        lax.all_gather(w_in, ("head", "blk"), axis=0, tiled=True),
        lax.all_gather(w_mlp_out, ("head", "blk"), axis=1, tiled=True),
    )
    gain_one = gain_one.astype(jnp.float32)
    gain_two = gain_two.astype(jnp.float32)
    blk_index = lax.axis_index("blk")
    own_rows = (lax.axis_index("head") * cycle_size + blk_index) * rows_dev + lax.iota(
        jnp.int32, rows_dev
    )
    segment, position = locate(own_rows, lengths)
    valid = (segment < nseq_count).astype(jnp.float32)[:, None]

    def cycle_segments(first_row, row_count):
        flat_rows = first_row + lax.iota(jnp.int32, row_count)
        return locate(spread(flat_rows, rows_dev, group_rows, cycle_size), lengths)[0]

    x_float = layer_input.astype(jnp.float32)
    norm_one, normed_one, scale_one = norm_forward(x_float, gain_one)
    input_bf = norm_one.astype(jnp.bfloat16)
    qkv_all = jnp.dot(input_bf, wqkv_full, preferred_element_type=jnp.float32).reshape(
        rows_dev, 3, all_heads, DH
    )
    stacked = jnp.stack(
        [rotate(qkv_all[:, 0], position, 1.0), rotate(qkv_all[:, 1], position, 1.0), qkv_all[:, 2]],
        axis=1,
    )
    stacked = stacked.astype(jnp.bfloat16).reshape(rows_dev, 3, head_groups, local_width)
    regrouped = lax.all_to_all(stacked, "head", split_axis=2, concat_axis=0, tiled=True)
    queries = regrouped[:, 0, 0].reshape(group_rows, local_heads, DH)
    key_value = regrouped[:, 1:, 0]
    own_keys = key_value[:, 0].reshape(group_rows, local_heads, DH)
    own_values = key_value[:, 1].reshape(group_rows, local_heads, DH)
    query_seg = cycle_segments(blk_index * group_rows, group_rows)
    start_state = (
        jnp.full((local_heads, group_rows), MASK_FLOOR, jnp.float32),
        jnp.zeros((local_heads, group_rows), jnp.float32),
        jnp.zeros((group_rows, local_heads, DH), jnp.float32),
    )
    carried = start_state
    key_part = lax.all_gather(key_value, "blk", axis=0, tiled=True)
    row_count = key_part.shape[0]
    block_rows = block_size(row_count, group_rows)
    key_seg = cycle_segments(jnp.int32(0), row_count)

    def attend_one_step(inner, block_at):
        part_rows = take_rows(key_part, block_at, block_rows)
        part_seg = take_rows(key_seg, block_at, block_rows)
        keys_in = part_rows[:, 0].reshape(block_rows, local_heads, DH)
        values_in = part_rows[:, 1].reshape(block_rows, local_heads, DH)
        return (online(inner, queries, keys_in, values_in, query_seg, part_seg), None)

    carried, ignored = lax.scan(
        attend_one_step, carried, lax.iota(jnp.int32, row_count // block_rows)
    )
    top_score, row_total, weighted = carried
    log_total = top_score + jnp.log(row_total)
    attended = weighted / row_total.T[:, :, None]
    attended_bf = attended.reshape(group_rows, local_width).astype(jnp.bfloat16)
    mixed = lax.all_to_all(attended_bf, "head", split_axis=0, concat_axis=1, tiled=True)
    attn_out = jnp.dot(mixed, wout_full, preferred_element_type=jnp.float32)
    hidden = x_float + attn_out
    norm_two, normed_two, scale_two = norm_forward(hidden, gain_two)
    middle_bf = norm_two.astype(jnp.bfloat16)
    gate_up = jnp.dot(middle_bf, win_full, preferred_element_type=jnp.float32)
    ff_width = gate_up.shape[1] // 2
    gate_part = gate_up[:, :ff_width]
    up_part = gate_up[:, ff_width:]
    gelu_gate, gelu_pull = jax.vjp(
        lambda gate_in: jax.nn.gelu(gate_in, approximate=False), gate_part
    )
    product = (gelu_gate * up_part).astype(jnp.bfloat16)
    mlp_out = jnp.dot(product, wdown_full, preferred_element_type=jnp.float32)
    y_out = valid * (hidden + mlp_out)
    grad_out = (out_grad.astype(jnp.float32) * valid).astype(jnp.bfloat16)
    grad_down = jnp.dot(product.T, grad_out, preferred_element_type=jnp.float32)
    grad_product = jnp.dot(grad_out, wdown_full.T, preferred_element_type=jnp.float32)
    grad_gate = gelu_pull(grad_product * up_part)[0]
    grad_gate_up = jnp.concatenate([grad_gate, grad_product * gelu_gate], axis=1).astype(
        jnp.bfloat16
    )
    grad_win = jnp.dot(middle_bf.T, grad_gate_up, preferred_element_type=jnp.float32)
    grad_middle = jnp.dot(grad_gate_up, win_full.T, preferred_element_type=jnp.float32)
    grad_hidden_ln, grad_gain_two = norm_backward(grad_middle, gain_two, normed_two, scale_two)
    grad_hidden = grad_out.astype(jnp.float32) + grad_hidden_ln
    grad_attn_bf = grad_hidden.astype(jnp.bfloat16)
    grad_wout = jnp.dot(mixed.T, grad_attn_bf, preferred_element_type=jnp.float32)
    grad_mixed = jnp.dot(grad_attn_bf, wout_full.T, preferred_element_type=jnp.float32).astype(
        jnp.bfloat16
    )
    grad_heads = lax.all_to_all(
        grad_mixed, "head", split_axis=1, concat_axis=0, tiled=True
    ).reshape(group_rows, local_heads, DH)
    row_delta = jnp.sum(grad_heads.astype(jnp.float32) * attended, axis=-1).T
    zero_grad = jnp.zeros((group_rows, local_heads, DH), jnp.float32)
    total_grad = zero_grad
    query_key_part = lax.all_gather(key_value, "blk", axis=0, tiled=True)
    row_count = query_key_part.shape[0]
    query_block_rows = block_size(row_count, group_rows)
    query_key_seg = cycle_segments(jnp.int32(0), row_count)

    def query_one_step(inner, block_at):
        part_rows = take_rows(query_key_part, block_at, query_block_rows)
        part_seg = take_rows(query_key_seg, block_at, query_block_rows)
        keys_in = part_rows[:, 0].reshape(query_block_rows, local_heads, DH)
        values_in = part_rows[:, 1].reshape(query_block_rows, local_heads, DH)
        probs, grad_scores = score_grads(
            queries, keys_in, values_in, grad_heads, log_total, row_delta, query_seg, part_seg
        )
        return (
            inner
            + 0.125
            * jnp.einsum("hqk,khd->qhd", grad_scores, keys_in, preferred_element_type=jnp.float32),
            None,
        )

    total_grad, ignored = lax.scan(
        query_one_step, total_grad, lax.iota(jnp.int32, row_count // query_block_rows)
    )
    carried = (zero_grad, zero_grad)
    query_rows = lax.all_gather(queries.astype(jnp.float32), "blk", axis=0, tiled=True)
    grad_rows = lax.all_gather(grad_heads.astype(jnp.float32), "blk", axis=0, tiled=True)
    lse_rows = lax.all_gather(log_total.T, "blk", axis=0, tiled=True)
    delta_rows = lax.all_gather(row_delta.T, "blk", axis=0, tiled=True)
    row_count = query_rows.shape[0]
    gather_block_rows = block_size(row_count, group_rows)
    seg_rows = cycle_segments(jnp.int32(0), row_count)

    def gather_one_step(inner, block_at):
        grad_keys, grad_values = key_grad_rows(
            take_rows(query_rows, block_at, gather_block_rows).astype(jnp.bfloat16),
            take_rows(grad_rows, block_at, gather_block_rows).astype(jnp.bfloat16),
            take_rows(lse_rows, block_at, gather_block_rows).T,
            take_rows(delta_rows, block_at, gather_block_rows).T,
            take_rows(seg_rows, block_at, gather_block_rows),
            own_keys,
            own_values,
            query_seg,
        )
        return ((inner[0] + grad_keys, inner[1] + grad_values), None)

    carried, ignored = lax.scan(
        gather_one_step, carried, lax.iota(jnp.int32, row_count // gather_block_rows)
    )
    grad_keys_all, grad_values_all = carried
    grad_stack = jnp.stack(
        [
            total_grad.reshape(group_rows, local_width),
            grad_keys_all.reshape(group_rows, local_width),
            grad_values_all.reshape(group_rows, local_width),
        ],
        axis=1,
    )
    grad_stack = grad_stack.astype(jnp.bfloat16).reshape(group_rows, 3, 1, local_width)
    grad_tokens = (
        lax.all_to_all(grad_stack, "head", split_axis=0, concat_axis=2, tiled=True)
        .reshape(rows_dev, 3, all_heads, DH)
        .astype(jnp.float32)
    )
    grad_qkv = jnp.stack(
        [
            rotate(grad_tokens[:, 0], position, -1.0),
            rotate(grad_tokens[:, 1], position, -1.0),
            grad_tokens[:, 2],
        ],
        axis=1,
    )
    grad_qkv = grad_qkv.reshape(rows_dev, 3 * width).astype(jnp.bfloat16)
    grad_wqkv = jnp.dot(input_bf.T, grad_qkv, preferred_element_type=jnp.float32)
    grad_input = jnp.dot(grad_qkv, wqkv_full.T, preferred_element_type=jnp.float32)
    grad_x_ln, grad_gain_one = norm_backward(grad_input, gain_one, normed_one, scale_one)
    dx_out = grad_hidden + grad_x_ln
    summed = (
        lax.psum_scatter(grad_gain_one, ("head", "blk"), scatter_dimension=0, tiled=True),
        lax.psum_scatter(grad_wqkv, ("head", "blk"), scatter_dimension=0, tiled=True),
        lax.psum_scatter(grad_wout, ("head", "blk"), scatter_dimension=0, tiled=True),
        lax.psum_scatter(grad_gain_two, ("head", "blk"), scatter_dimension=0, tiled=True),
        lax.psum_scatter(grad_win, ("head", "blk"), scatter_dimension=0, tiled=True),
        lax.psum_scatter(grad_down, ("head", "blk"), scatter_dimension=1, tiled=True),
    )
    return (y_out, dx_out, summed[0], summed[1], summed[2], summed[3], summed[4], summed[5])


def solution(mesh):
    return jax.shard_map(
        shards,
        mesh=mesh,
        in_specs=(
            P(("head", "blk"), None),
            P(("head", "blk"), None),
            P(),
            P(("head", "blk")),
            P(("head", "blk"), None),
            P(("head", "blk"), None),
            P(("head", "blk")),
            P(("head", "blk"), None),
            P(None, ("head", "blk")),
        ),
        out_specs=(
            P(("head", "blk"), None),
            P(("head", "blk"), None),
            P(("head", "blk")),
            P(("head", "blk"), None),
            P(("head", "blk"), None),
            P(("head", "blk")),
            P(("head", "blk"), None),
            P(None, ("head", "blk")),
        ),
        check_vma=False,
    )
```

profile of v0, /device:TPU:0, one launch (start us, length us, event | category | flops | bytes accessed | tf_op | source)
XLA Modules:
  0.0 1424.9 jit_solution(2221315387794891188)
XLA Ops:
  9.7 43.0 %all-reduce.5 = (bf16[1024]{0:T(1024)(128)(2,1)S(1)}, bf16[1024]{0:T(1024)(128)(2,1)S(1)}) all-reduce(bf16[1024]{0:T(1024)(128)(2,1)S(1)} %dynamic-update-slice, bf16[1024]{0:T(1024)(128)(2,1)S(1)} %dynamic-update-slice.1), channel_id=1, replica_groups=mesh['head'=4,'blk'=8] {'head','blk'}, use_global_device_ids=true, to_apply=%add | all-reduce | flops 2048 | bytes 8192
  58.1 25.4 %all-gather.9.cloned.1.call-done = bf16[1024,3072]{1,0:T(8,128)(2,1)} async-done(((bf16[32,3072]{1,0:T(8,128)(2,1)}), bf16[1024,3072]{1,0:T(8,128)(2,1)}) %all-gather.9.cloned.1.call-update) | async-done | bytes 6291472 | tf_op jit(solution)/shard_map/all_gather | solution.py:120
  83.5 5.5 fusion.107
  89.5 14.1 all_to_all.59
  107.2 69.6 %all-gather.21.cloned.1.call-done = bf16[4096,2,1,256]{3,0,1,2:T(8,128)(2,1)} async-done(((bf16[512,2,1,256]{3,0,1,2:T(8,128)(2,1)}), bf16[4096,2,1,256]{3,0,1,2:T(8,128)(2,1)}) %all-gather.21.cloned.1.call-update) | async-done | bytes 4194320 | tf_op jit(solution)/shard_map/all_gather | solution.py:162
  176.8 6.4 copy.132
  183.2 83.1 %while.39 = (s32[]{:T(128)}, f32[4,512]{1,0:T(4,128)S(1)}, f32[4,512]{1,0:T(4,128)S(1)}, f32[512,4,64]{0,2,1:T(8,128)S(1)}, s32[512]{0:T(512)S(1)}, /*index=5*/s...) while((s32[]{:T(128)}, f32[4,512]{1,0:T(4,128)S(1)}, ...), condition=%wide.region_10.11_spmd.clone, body=%wide.region_7.10_spmd.clone.sunk | while | flops 282734592 | bytes 33431812 | solution.py:174
  271.8 6.3 all-to-all-done.1
  280.5 46.5 %all-gather.13.cloned.1.call-done = bf16[1024,5248]{1,0:T(8,128)(2,1)} async-done(((bf16[32,5248]{1,0:T(8,128)(2,1)}), bf16[1024,5248]{1,0:T(8,128)(2,1)}) %all-gather.13.cloned.1.call-update) | async-done | bytes 10747920 | tf_op jit(solution)/shard_map/all_gather | solution.py:123
  327.0 7.2 fusion.109
  334.2 60.3 %all-gather.15.cloned.1.call-done = bf16[2624,1024]{0,1:T(8,128)(2,1)} async-done(((bf16[2624,32]{0,1:T(8,128)(2,1)}), bf16[2624,1024]{0,1:T(8,128)(2,1)}) %all-gather.15.cloned.1.call-update) | async-done | bytes 5373968 | tf_op jit(solution)/shard_map/all_gather | solution.py:124
  394.5 7.3 add_convert_fusion
  408.0 9.1 all_to_all.60
  424.6 31.0 %all_gather.42 = f32[4096,4]{0,1:T(4,128)S(1)} all-gather(f32[512,4]{0,1:T(4,128)S(1)} %bitcast.236), channel_id=1, replica_groups=mesh['head'=4,'blk'=8] {'blk'}, dimensions={0}, use_global_device_ids=true | all-gather | bytes 73728 | tf_op jit(solution)/shard_map/all_gather | solution.py:244
  455.6 5.8 fusion.103
  463.5 30.7 %all_gather.44 = f32[4096,4]{0,1:T(4,128)S(1)} all-gather(f32[512,4]{0,1:T(4,128)S(1)} %multiply_reduce_fusion.1), channel_id=1, replica_groups=mesh['head'=4,'blk'=8] {'blk'}, dimensions={0}, use_global_device_ids=true | all-gather | bytes 73728 | tf_op jit(solution)/shard_map/all_gather | solution.py:245
  494.2 82.9 %while.40 = (s32[]{:T(128)}, f32[512,4,64]{0,2,1:T(8,128)}, s32[8]{0:T(128)S(1)}, bf16[4096,2,256]{0,2,1:T(8,128)(2,1)}, s32[512]{0:T(512)S(1)}, /*index=5*/s32[...) while((s32[]{:T(128)}, f32[512,4,64]{0,2,1:T(8,128)}, ...), condition=%wide.region_17.18_spmd.clone, body=%wide.region_16.17_spmd.clone.sunk | while | flops 409600000 | bytes 12345585 | solution.py:238
  499.5 4.9 fusion.175
  509.8 5.0 fusion.175
  520.2 5.0 fusion.175
  530.6 5.1 fusion.175
  541.0 5.0 fusion.175
  551.3 5.0 fusion.175
  561.7 5.0 fusion.175
  572.1 5.0 fusion.175
  578.3 116.8 %while.41 = (s32[]{:T(128)}, f32[512,4,64]{0,2,1:T(8,128)}, f32[512,4,64]{0,2,1:T(8,128)}, s32[8]{0:T(128)S(1)}, bf16[4096,4,64]{0,2,1:T(8,128)(2,1)}, /*index=5...) while((s32[]{:T(128)}, f32[512,4,64]{0,2,1:T(8,128)}, ...), condition=%wide.region_19.20_spmd.clone, body=%wide.region_18.19_spmd.clone.sunk | while | flops 548274176 | bytes 21301032 | solution.py:263
  588.0 4.5 fusion.181
  602.3 4.7 fusion.181
  612.3 4.5 fusion.180
  616.8 4.7 fusion.181
  626.7 4.5 fusion.180
  631.2 4.6 fusion.181
  641.2 4.5 fusion.180
  645.7 4.6 fusion.181
  655.6 4.8 fusion.180
  660.4 4.9 fusion.181
  670.6 4.7 fusion.180
  675.3 4.9 fusion.181
  685.5 4.7 fusion.180
  690.3 4.8 fusion.181
  700.5 24.3 %all_to_all.61 = bf16[512,3,1,256]{3,1,2,0:T(4,128)(2,1)S(1)} all-to-all(bf16[512,3,1,256]{3,1,2,0:T(4,128)(2,1)} %copy.141), channel_id=1, replica_groups=mesh['head'=4,'blk'=8] {'head'}, dimensions={0} | all-to-all | bytes 1572864 | tf_op jit(solution)/shard_map/all_to_all | solution.py:277
  731.8 6.5 fusion.105
  739.4 10.3 fusion.56
  750.3 5.3 fusion.55
  755.7 5.7 fusion.69
  761.4 39.6 %all-reduce.4 = (f32[1024]{0:T(1024)S(1)}, f32[1024]{0:T(1024)S(1)}) all-reduce(f32[1024]{0:T(1024)S(1)} %get-tuple-element.440, f32[1024]{0:T(1024)S(1)} %copy-done.19), channel_id=3, replica_groups=mesh['head'=4,'blk'=8] {'head','blk'}, use_global_device_ids=true, to_apply=%region_23.24.clone | all-reduce | flops 2048 | bytes 16384
  803.2 157.4 %reduce-scatter.5.cloned.1.call-done = f32[32,3072]{1,0:T(8,128)} async-done(((f32[1024,3072]{1,0:T(8,128)}), f32[32,3072]{1,0:T(8,128)}) %reduce-scatter.5.cloned.1.call-update) | async-done | bytes 393232 | tf_op jit(solution)/shard_map/reduce_scatter | solution.py:296
  960.7 457.5 %reduce-scatter.9.cloned.1.call-done = f32[32,5248]{1,0:T(8,128)} async-done(((f32[1024,5248]{1,0:T(8,128)}), f32[32,5248]{1,0:T(8,128)}) %reduce-scatter.9.cloned.1.call-update) | async-done | bytes 671760 | tf_op jit(solution)/shard_map/reduce_scatter | solution.py:299
  (357 shorter events, 213.3 us)
Async XLA Ops:
  7.2 76.3 %all-gather.9.cloned.1.call-start = ((), (), s32[]{:S(2)}) async-start(), calls=%async_computation.8 | async-start | bytes 6488064 | tf_op jit(solution)/shard_map/all_gather | solution.py:120
  7.9 168.9 %all-gather.21.cloned.1.call-start = ((), (), s32[]{:S(2)}) async-start(), calls=%async_computation.18 | async-start | bytes 4718592 | tf_op jit(solution)/shard_map/all_gather | solution.py:162
  104.9 166.9 %all-gather.11.cloned.1.call-start = ((), (), s32[]{:S(2)}) async-start(), calls=%async_computation.9 | async-start | bytes 2162688 | tf_op jit(solution)/shard_map/all_gather | solution.py:121
  105.6 221.4 %all-gather.13.cloned.1.call-start = ((), (), s32[]{:S(2)}) async-start(), calls=%async_computation.10 | async-start | bytes 11083776 | tf_op jit(solution)/shard_map/all_gather | solution.py:123
  106.2 288.3 %all-gather.15.cloned.1.call-start = ((), (), s32[]{:S(2)}) async-start(), calls=%async_computation.11 | async-start | bytes 5677056 | tf_op jit(solution)/shard_map/all_gather | solution.py:124
  188.7 3.5 copy-start
  199.1 3.5 copy-start
  209.4 3.5 copy-start
  219.7 3.5 copy-start
  230.1 3.6 copy-start
  240.5 3.5 copy-start
  250.9 3.5 copy-start
  261.2 3.7 copy-start
  266.3 4.4 copy-start.1
  266.3 13.9 copy-start.11
  266.3 11.8 copy-start.4
  267.2 10.9 all-to-all-start.1
  270.6 307.6 %all-gather.17.cloned.1.call-start = ((), (), s32[]{:S(2)}) async-start(), calls=%async_computation.12 | async-start | bytes 2359296 | tf_op jit(solution)/shard_map/all_gather | solution.py:242
  270.7 184.9 %copy-start.17 = (f32[128]{0:T(128)}, f32[128]{0:T(128)S(1)}, u32[]{:S(2)}) copy-start(f32[128]{0:T(128)S(1)} %compare_convert_fusion) | copy-start | bytes 1540
  271.2 307.0 %all-gather.19.cloned.1.call-start = ((), (), s32[]{:S(2)}) async-start(), calls=%async_computation.13 | async-start | bytes 2359296 | tf_op jit(solution)/shard_map/all_gather | solution.py:243
  280.5 114.0 %copy-start.13 = (bf16[128,1024]{1,0:T(8,128)(2,1)S(1)}, bf16[128,1024]{1,0:T(8,128)(2,1)}, u32[]{:S(2)}) copy-start(bf16[128,1024]{1,0:T(8,128)(2,1)} %param.16) | copy-start | bytes 786436
  394.5 7.3 copy-start.5
  394.5 8.2 copy-start.3
  402.3 4.5 copy-start.9
  402.7 4.5 copy-start.6
  419.1 384.1 %reduce-scatter.7.cloned.1.call-start = ((), (), s32[]{:S(2)}) async-start(), calls=%async_computation.15 | async-start | bytes 4325376 | tf_op jit(solution)/shard_map/reduce_scatter | solution.py:297
  421.8 381.4 %reduce-scatter.11.cloned.1.call-start = ((), (), s32[]{:S(2)}) async-start(), calls=%async_computation.17 | async-start | bytes 11354112 | tf_op jit(solution)/shard_map/reduce_scatter | solution.py:300
  461.4 32.8 %copy-start.2 = (bf16[512,4,64]{0,2,1:T(8,128)(2,1)S(1)}, bf16[512,4,64]{0,2,1:T(8,128)(2,1)}, u32[]{:S(2)}) copy-start(bf16[512,4,64]{0,2,1:T(8,128)(2,1)} %copy-done.1) | copy-start | bytes 786436
  461.4 499.2 %reduce-scatter.5.cloned.1.call-start = ((), (), s32[]{:S(2)}) async-start(), calls=%async_computation.14 | async-start | bytes 12976128 | tf_op jit(solution)/shard_map/reduce_scatter | solution.py:296
  579.5 4.0 copy-start.15
  588.0 4.5 copy-start.16
  593.8 4.0 copy-start.15
  602.3 4.7 copy-start.16
  608.2 4.0 copy-start.15
  616.8 4.7 copy-start.16
  622.7 4.0 copy-start.15
  631.2 4.7 copy-start.16
  637.1 4.0 copy-start.15
  645.7 4.7 copy-start.16
  651.6 4.0 copy-start.15
  660.4 4.9 copy-start.16
  666.5 4.0 copy-start.15
  675.3 4.9 copy-start.16
  681.5 4.0 copy-start.15
  690.3 4.8 copy-start.16
  738.3 679.9 %reduce-scatter.9.cloned.1.call-start = ((), (), s32[]{:S(2)}) async-start(), calls=%async_computation.16 | async-start | bytes 22167552 | tf_op jit(solution)/shard_map/reduce_scatter | solution.py:299
  750.3 5.3 copy-start.8
  755.7 5.8 copy-start.19
  (5 other events, 4.6 us)
Sparse Core Ops, SparseCore 0:
  10.9 72.5 all-gather.8
  105.0 71.7 all-gather.20
  179.8 54.8 all-gather.10
  237.4 89.5 all-gather.12
  329.8 64.6 all-gather.14
  397.0 50.7 all-gather.16
  449.8 50.5 all-gather.18
  503.3 141.4 reduce-scatter.6
  651.3 148.2 reduce-scatter.10
  806.0 154.5 reduce-scatter.4
  963.6 454.4 reduce-scatter.8
where the time goes:
time: 1430 us; the launch traced here: 1420 us
  waiting for transfers between devices  826 us (58%)
  matrix products  263 us (18%)
  blocking collectives  192 us (13%)
  local copies, waits for them, and re-layouts  61.3 us (4%)
  other arithmetic  46.9 us (3%)
  loops' own time  16.5 us (1%)
  between operations  14.6 us (1%)
    reduce_scatter x1, waiting for transfers between devices, shards(): lax.psum_scatter(grad_win, ('head', 'blk'), scatter_dimension=0, tiled=True)  458 us
    reduce_scatter x1, waiting for transfers between devices, shards(): lax.psum_scatter(grad_wqkv, ('head', 'blk'), scatter_dimension=0, tiled=T...  157 us
    unnamed x2, blocking collectives  82.6 us
    all_gather x1, waiting for transfers between devices, shards(): key_part = lax.all_gather(key_value, 'blk', axis=0, tiled=True)  69.6 us
    all_gather x1, waiting for transfers between devices, shards(): lax.all_gather(w_mlp_out, ('head', 'blk'), axis=1, tiled=True)  60.3 us
    dot_general x16, matrix products, score_grads(): jnp.einsum('qhd,khd->hqk', query_in, key_in, preferred_element_type=jnp.f...  51.3 us
    all_gather x1, waiting for transfers between devices, shards(): lax.all_gather(w_in, ('head', 'blk'), axis=0, tiled=True)  46.5 us
    dot_general x8, matrix products, query_one_step(): jnp.einsum('hqk,khd->qhd', grad_scores, keys_in, preferred_element_type=j...  40.1 us
  transfers between devices with their start and end apart: 12, of which 7 were waited for; matrix products, arithmetic and copies ran while one was open for 25% of the time, Pallas kernels for 0%

commit v1 on v0

--- a/solution.py
+++ b/solution.py
@@ -7,6 +7,18 @@
 ROPE_BASE = 160000.0
 NORM_EPS = 1e-05
 MASK_FLOOR = -1e30
+
+
+def gather_by_bits(x, axis, dim):
+    ways, here = (lax.axis_size(axis), lax.axis_index(axis))
+    grown, reach = (x, 1)
+    while reach < ways:
+        theirs = lax.ppermute(grown, axis, [(d, d ^ reach) for d in range(ways)])
+        mine_first = jnp.concatenate([grown, theirs], axis=dim)
+        theirs_first = jnp.concatenate([theirs, grown], axis=dim)
+        grown = jnp.where(here & reach == 0, mine_first, theirs_first)
+        reach = 2 * reach
+    return grown
 
 
 def norm_forward(values, gain):
@@ -121,7 +133,7 @@
         lax.all_gather(w_attn_out, ("head", "blk"), axis=0, tiled=True),
         lax.all_gather(ln_mlp, ("head", "blk"), axis=0, tiled=True),
         lax.all_gather(w_in, ("head", "blk"), axis=0, tiled=True),
-        lax.all_gather(w_mlp_out, ("head", "blk"), axis=1, tiled=True),
+        gather_by_bits(w_mlp_out, ("head", "blk"), 1),
     )
     gain_one = gain_one.astype(jnp.float32)
     gain_two = gain_two.astype(jnp.float32)

time: 1430 us -> 1390 us (0.972)
  waiting for transfers between devices: 826 us -> 755 us
  local copies, waits for them, and re-layouts: 61.3 us -> 99.6 us
    ppermute x0 -> x5, waiting for transfers between devices: none -> 74 us  [gather_by_bits(): theirs = lax.ppermute(grown, axis, [(d, d ^ reach) for d in range(ways)])]
    all_gather x1, waiting for transfers between devices: 69.6 us -> 2.16 us  [shards(): key_part = lax.all_gather(key_value, 'blk', axis=0, tiled=True)]
    all_gather x1 -> x0, waiting for transfers between devices: 60.3 us -> none  [shards(): lax.all_gather(w_mlp_out, ('head', 'blk'), axis=1, tiled=True)]
    dynamic_slice x24, local copies, waits for them, and re-layouts: 1.81 us -> 18 us  [take_rows(): lax.dynamic_slice_in_dim(array_in, block_at * block_rows, block_rows, 0)]
  transfers between devices with their start and end apart: 12 -> 16, of which waited for: 7 -> 10; matrix products, arithmetic and copies ran while one was open for 25% -> 27% of each run, Pallas kernels for 0% -> 0%
where the time goes in v1:
time: 1390 us; the launch traced here: 1380 us
  waiting for transfers between devices  755 us (54%)
  matrix products  249 us (18%)
  blocking collectives  189 us (14%)
  local copies, waits for them, and re-layouts  99.6 us (7%)
  other arithmetic  50.1 us (4%)
  loops' own time  16.3 us (1%)
  between operations  15.3 us (1%)
    reduce_scatter x1, waiting for transfers between devices, shards(): lax.psum_scatter(grad_win, ('head', 'blk'), scatter_dimension=0, tiled=True)  457 us
    reduce_scatter x1, waiting for transfers between devices, shards(): lax.psum_scatter(grad_wqkv, ('head', 'blk'), scatter_dimension=0, tiled=T...  147 us
    unnamed x2, blocking collectives  80.5 us
    ppermute x5, waiting for transfers between devices, gather_by_bits(): theirs = lax.ppermute(grown, axis, [(d, d ^ reach) for d in range(ways)])  74 us
    dot_general x16, matrix products, score_grads(): jnp.einsum('qhd,khd->hqk', query_in, key_in, preferred_element_type=jnp.f...  51.6 us
    all_gather x1, waiting for transfers between devices, shards(): lax.all_gather(w_in, ('head', 'blk'), axis=0, tiled=True)  46.5 us
    dot_general x8, matrix products, query_one_step(): jnp.einsum('hqk,khd->qhd', grad_scores, keys_in, preferred_element_type=j...  39.6 us
    dot_general x8, matrix products, key_grad_rows(): jnp.einsum('hqk,qhd->khd', grad_scores, query_in, preferred_element_type=...  36.2 us
  transfers between devices with their start and end apart: 16, of which 10 were waited for; matrix products, arithmetic and copies ran while one was open for 27% of the time, Pallas kernels for 0%

profile of v1, /device:TPU:0, one launch (start us, length us, event | category | flops | bytes accessed | tf_op | source)
XLA Modules:
  0.0 1383.1 jit_solution(16577572526171363719)
XLA Ops:
  9.7 43.0 %all-reduce.5 = (bf16[1024]{0:T(1024)(128)(2,1)S(1)}, bf16[1024]{0:T(1024)(128)(2,1)S(1)}) all-reduce(bf16[1024]{0:T(1024)(128)(2,1)S(1)} %dynamic-update-slice, bf16[1024]{0:T(1024)(128)(2,1)S(1)} %dynamic-update-slice.1), channel_id=1, replica_groups=mesh['head'=4,'blk'=8] {'head','blk'}, use_global_device_ids=true, to_apply=%add | all-reduce | flops 2048 | bytes 8192
  58.7 24.8 %all-gather.8.cloned.1.call-done = bf16[1024,3072]{1,0:T(8,128)(2,1)} async-done(((bf16[32,3072]{1,0:T(8,128)(2,1)}), bf16[1024,3072]{1,0:T(8,128)(2,1)}) %all-gather.8.cloned.1.call-update) | async-done | bytes 6291472 | tf_op jit(solution)/shard_map/all_gather | solution.py:132
  83.5 5.5 fusion.109
  89.6 14.1 %all_to_all.59 = bf16[128,3,4,256]{0,3,1,2:T(8,128)(2,1)S(1)} all-to-all(bf16[128,3,4,256]{0,3,1,2:T(8,128)(2,1)S(1)} %copy.144), channel_id=1, replica_groups=mesh['head'=4,'blk'=8] {'head'}, dimensions={2} | all-to-all | bytes 1572864 | tf_op jit(solution)/shard_map/all_to_all | solution.py:162
  107.9 4.3 collective-permute-done
  113.9 22.6 %collective-permute-done.1 = bf16[2624,64]{0,1:T(8,128)(2,1)S(1)} collective-permute-done((bf16[2624,64]{0,1:T(8,128)(2,1)S(1)}, bf16[2624,64]{0,1:T(8,128)(2,1)S(1)}, u32[]{:S(2)}, u32[]{:S(2)}) %collective-permute-start.1) | collective-permute-done | bytes 335904 | tf_op jit(solution)/shard_map/ppermute | solution.py:16
  137.0 44.8 %collective-permute-done.2 = bf16[2624,128]{1,0:T(8,128)(2,1)S(1)} collective-permute-done((bf16[2624,128]{1,0:T(8,128)(2,1)S(1)}, bf16[2624,128]{1,0:T(8,128)(2,1)S(1)}, u32[]{:S(2)}, u32[]{:S(2)}) %collective-permute-start.2) | collective-permute-done | bytes 671776 | tf_op jit(solution)/shard_map/ppermute | solution.py:16
  188.3 4.3 maximum_select_fusion.1
  192.6 4.6 copy.155
  200.9 6.5 copy.147
  207.3 88.5 %while.39 = (s32[]{:T(128)}, f32[4,512]{1,0:T(4,128)S(1)}, f32[4,512]{1,0:T(4,128)S(1)}, f32[512,4,64]{0,2,1:T(8,128)S(1)}, s32[512]{0:T(512)S(1)}, /*index=5*/s...) while((s32[]{:T(128)}, f32[4,512]{1,0:T(4,128)S(1)}, ...), condition=%wide.region_10.11_spmd.clone, body=%wide.region_7.10_spmd.clone.sunk | while | flops 282734592 | bytes 33431812 | solution.py:186
  300.3 4.5 copy.156
  309.4 46.5 %all-gather.12.cloned.1.call-done = bf16[1024,5248]{1,0:T(8,128)(2,1)} async-done(((bf16[32,5248]{1,0:T(8,128)(2,1)}), bf16[1024,5248]{1,0:T(8,128)(2,1)}) %all-gather.12.cloned.1.call-update) | async-done | bytes 10747920 | tf_op jit(solution)/shard_map/all_gather | solution.py:135
  355.9 5.9 fusion.111
  361.8 6.0 add_convert_fusion
  369.0 4.2 multiply_reduce_fusion
  374.4 8.5 all_to_all.60
  390.4 30.9 %all_gather.38 = f32[4096,4]{0,1:T(4,128)S(1)} all-gather(f32[512,4]{0,1:T(4,128)S(1)} %bitcast.238), channel_id=1, replica_groups=mesh['head'=4,'blk'=8] {'blk'}, dimensions={0}, use_global_device_ids=true | all-gather | bytes 73728 | tf_op jit(solution)/shard_map/all_gather | solution.py:256
  421.3 5.7 fusion.106
  428.3 32.7 %all_gather.40 = f32[4096,4]{0,1:T(4,128)} all-gather(f32[512,4]{0,1:T(4,128)S(1)} %multiply_reduce_fusion.1), channel_id=1, replica_groups=mesh['head'=4,'blk'=8] {'blk'}, dimensions={0}, use_global_device_ids=true | all-gather | bytes 73728 | tf_op jit(solution)/shard_map/all_gather | solution.py:257
  460.9 87.0 %while.40 = (s32[]{:T(128)}, f32[512,4,64]{0,2,1:T(8,128)}, s32[8]{0:T(128)S(1)}, bf16[4096,2,256]{0,2,1:T(8,128)(2,1)}, s32[512]{0:T(512)S(1)}, /*index=5*/s32[...) while((s32[]{:T(128)}, f32[512,4,64]{0,2,1:T(8,128)}, ...), condition=%wide.region_17.18_spmd.clone, body=%wide.region_16.17_spmd.clone.sunk | while | flops 409600000 | bytes 12345585 | solution.py:250
  466.9 4.8 fusion.175
  477.6 5.0 fusion.175
  488.6 4.9 fusion.175
  499.4 5.0 fusion.175
  510.3 5.0 fusion.175
  521.2 5.0 fusion.175
  532.1 4.9 fusion.175
  543.0 5.0 fusion.175
  549.1 125.4 %while.41 = (s32[]{:T(128)}, f32[512,4,64]{0,2,1:T(8,128)S(1)}, f32[512,4,64]{0,2,1:T(8,128)}, s32[8]{0:T(128)S(1)}, bf16[4096,4,64]{0,2,1:T(8,128)(2,1)}, /*ind...) while((s32[]{:T(128)}, f32[512,4,64]{0,2,1:T(8,128)S(1)}, ...), condition=%wide.region_19.20_spmd.clone, body=%wide.region_18.19_spmd.clone.sunk | while | flops 548274176 | bytes 22349636 | solution.py:275
  555.8 4.4 fusion.180
  571.3 4.4 fusion.180
  586.9 4.5 fusion.180
  602.4 4.5 fusion.180
  617.9 4.7 fusion.180
  622.6 3.8 fusion.181
  633.9 4.7 fusion.180
  638.6 3.8 fusion.181
  644.5 3.7 fusion.179
  650.0 4.6 fusion.180
  665.7 4.4 fusion.180
  678.2 22.5 %all_to_all.61 = bf16[512,3,1,256]{3,1,2,0:T(4,128)(2,1)S(1)} all-to-all(bf16[512,3,1,256]{3,1,2,0:T(4,128)(2,1)S(1)} %copy.165), channel_id=1, replica_groups=mesh['head'=4,'blk'=8] {'head'}, dimensions={0} | all-to-all | bytes 1572864 | tf_op jit(solution)/shard_map/all_to_all | solution.py:289
  705.3 6.5 fusion.107
  713.1 9.2 fusion.57
  722.9 7.3 fusion.55
  732.5 37.4 %all-reduce.4 = (f32[1024]{0:T(1024)S(1)}, f32[1024]{0:T(1024)S(1)}) all-reduce(f32[1024]{0:T(1024)S(1)} %get-tuple-element.440, f32[1024]{0:T(1024)S(1)} %copy-done.42), channel_id=3, replica_groups=mesh['head'=4,'blk'=8] {'head','blk'}, use_global_device_ids=true, to_apply=%region_23.24.clone | all-reduce | flops 2048 | bytes 16384
  772.2 146.5 %reduce-scatter.5.cloned.1.call-done = f32[32,3072]{1,0:T(8,128)} async-done(((f32[1024,3072]{1,0:T(8,128)}), f32[32,3072]{1,0:T(8,128)}) %reduce-scatter.5.cloned.1.call-update) | async-done | bytes 393232 | tf_op jit(solution)/shard_map/reduce_scatter | solution.py:308
  918.7 457.3 %reduce-scatter.9.cloned.1.call-done = f32[32,5248]{1,0:T(8,128)} async-done(((f32[1024,5248]{1,0:T(8,128)}), f32[32,5248]{1,0:T(8,128)}) %reduce-scatter.9.cloned.1.call-update) | async-done | bytes 671760 | tf_op jit(solution)/shard_map/reduce_scatter | solution.py:311
  (458 shorter events, 258.1 us)
Async XLA Ops:
  7.2 76.4 %all-gather.8.cloned.1.call-start = ((), (), s32[]{:S(2)}) async-start(), calls=%async_computation.8 | async-start | bytes 6488064 | tf_op jit(solution)/shard_map/all_gather | solution.py:132
  7.9 192.9 %all-gather.18.cloned.1.call-start = ((), (), s32[]{:S(2)}) async-start(), calls=%async_computation.17 | async-start | bytes 4718592 | tf_op jit(solution)/shard_map/all_gather | solution.py:174
  52.7 36.4 %copy-start.26 = (f32[1024]{0:T(1024)}, f32[1024]{0:T(1024)S(1)}, u32[]{:S(2)}) copy-start(f32[1024]{0:T(1024)S(1)} %convert_element_type.125) | copy-start | bytes 12292
  56.8 32.3 %copy-start.35 = (f32[128]{0:T(128)}, f32[128]{0:T(128)S(1)}, u32[]{:S(2)}) copy-start(f32[128]{0:T(128)S(1)} %broadcast_multiply_fusion.6) | copy-start | bytes 1540
  57.9 31.1 %copy-start.39 = (f32[128]{0:T(128)}, f32[128]{0:T(128)S(1)}, u32[]{:S(2)}) copy-start(f32[128]{0:T(128)S(1)} %add_rsqrt_fusion.1) | copy-start | bytes 1540
  58.7 30.5 %copy-start.30 = (f32[128,32]{0,1:T(8,128)}, f32[128,32]{0,1:T(8,128)S(1)}, u32[]{:S(2)}) copy-start(f32[128,32]{0,1:T(8,128)S(1)} %get-tuple-element.546) | copy-start | bytes 49156
  105.1 200.0 %all-gather.10.cloned.1.call-start = ((), (), s32[]{:S(2)}) async-start(), calls=%async_computation.9 | async-start | bytes 2162688 | tf_op jit(solution)/shard_map/all_gather | solution.py:133
  105.9 250.1 %all-gather.12.cloned.1.call-start = ((), (), s32[]{:S(2)}) async-start(), calls=%async_computation.10 | async-start | bytes 11083776 | tf_op jit(solution)/shard_map/all_gather | solution.py:135
  106.4 5.8 collective-permute-start
  112.3 24.2 %collective-permute-start.1 = (bf16[2624,64]{0,1:T(8,128)(2,1)S(1)}, bf16[2624,64]{0,1:T(8,128)(2,1)S(1)}, u32[]{:S(2)}, u32[]{:S(2)}) collective-permute-start(bf16[2624,64]{0,1:T(8,128)(2,1)S(1)} %maximum_select_fusion.6), channel_id=1, source_target_pairs={{0,2},{1,3},{2,0},{3,1},{4,6},{5,7},{6,4},{7,5},{8,10},{9,11},{10,... | collective-permute-start | bytes 1007624 | tf_op jit(solution)/shard_map/ppermute | solution.py:16
  136.9 44.9 %collective-permute-start.2 = (bf16[2624,128]{1,0:T(8,128)(2,1)S(1)}, bf16[2624,128]{1,0:T(8,128)(2,1)S(1)}, u32[]{:S(2)}, u32[]{:S(2)}) collective-permute-start(bf16[2624,128]{1,0:T(8,128)(2,1)S(1)} %copy.149), channel_id=1, source_target_pairs={{0,4},{1,5},{2,6},{3,7},{4,0},{5,1},{6,2},{7,3},{8,12},{9,13},{10,... | collective-permute-start | bytes 2015240 | tf_op jit(solution)/shard_map/ppermute | solution.py:16
  183.3 3.3 collective-permute-start.3
  197.2 103.1 %collective-permute-start.4 = (bf16[2624,512]{1,0:T(8,128)(2,1)}, bf16[2624,512]{1,0:T(8,128)(2,1)}, u32[]{:S(2)}, u32[]{:S(2)}) collective-permute-start(bf16[2624,512]{1,0:T(8,128)(2,1)} %copy.155), channel_id=1, source_target_pairs={{0,16},{1,17},{2,18},{3,19},{4,20},{5,21},{6,22},{7,23},{8,24},{9,... | collective-permute-start | bytes 8060936 | tf_op jit(solution)/shard_map/ppermute | solution.py:16
  200.8 6.5 copy-start.14
  200.9 6.5 copy-start.21
  295.8 9.0 copy-start.1
  295.9 9.0 copy-start.15
  296.8 10.2 all-to-all-start.1
  300.2 248.9 %all-gather.14.cloned.1.call-start = ((), (), s32[]{:S(2)}) async-start(), calls=%async_computation.11 | async-start | bytes 2359296 | tf_op jit(solution)/shard_map/all_gather | solution.py:254
  300.3 121.0 %copy-start.43 = (f32[128]{0:T(128)}, f32[128]{0:T(128)S(1)}, u32[]{:S(2)}) copy-start(f32[128]{0:T(128)S(1)} %compare_convert_fusion) | copy-start | bytes 1540
  300.3 6.7 copy-start.3
  304.9 244.2 %all-gather.16.cloned.1.call-start = ((), (), s32[]{:S(2)}) async-start(), calls=%async_computation.12 | async-start | bytes 2359296 | tf_op jit(solution)/shard_map/all_gather | solution.py:255
  309.2 64.0 %copy-start.33 = (f32[128]{0:T(128)}, f32[128]{0:T(128)S(1)}, u32[]{:S(2)}) copy-start(f32[128]{0:T(128)S(1)} %broadcast_multiply_fusion.5) | copy-start | bytes 1540
  309.4 63.8 %copy-start.37 = (f32[128]{0:T(128)}, f32[128]{0:T(128)S(1)}, u32[]{:S(2)}) copy-start(f32[128]{0:T(128)S(1)} %add_rsqrt_fusion) | copy-start | bytes 1540
  309.4 52.4 %copy-start.17 = (bf16[128,1024]{1,0:T(8,128)(2,1)S(1)}, bf16[128,1024]{1,0:T(8,128)(2,1)}, u32[]{:S(2)}) copy-start(bf16[128,1024]{1,0:T(8,128)(2,1)} %param.16) | copy-start | bytes 786436
  355.9 5.9 copy-start.4
  355.9 5.9 copy-start.11
  355.9 12.6 slice-start.2
  361.8 6.7 slice-start.3
  361.8 6.7 slice-start.4
  368.5 52.8 %copy-start.8 = (bf16[128,2624]{1,0:T(8,128)(2,1)}, bf16[128,2624]{1,0:T(8,128)(2,1)S(1)}, u32[]{:S(2)}) copy-start(bf16[128,2624]{1,0:T(8,128)(2,1)S(1)} %get-tuple-element.523) | copy-start | bytes 2015236
  383.9 388.3 %reduce-scatter.7.cloned.1.call-start = ((), (), s32[]{:S(2)}) async-start(), calls=%async_computation.14 | async-start | bytes 4325376 | tf_op jit(solution)/shard_map/reduce_scatter | solution.py:309
  386.6 34.7 %copy-start.18 = (bf16[128,1024]{1,0:T(8,128)(2,1)S(1)}, bf16[128,1024]{1,0:T(8,128)(2,1)}, u32[]{:S(2)}) copy-start(bf16[128,1024]{1,0:T(8,128)(2,1)} %param.16) | copy-start | bytes 786436
  386.7 385.5 %reduce-scatter.11.cloned.1.call-start = ((), (), s32[]{:S(2)}) async-start(), calls=%async_computation.16 | async-start | bytes 11354112 | tf_op jit(solution)/shard_map/reduce_scatter | solution.py:312
  427.0 33.9 %copy-start.2 = (bf16[512,4,64]{0,2,1:T(8,128)(2,1)S(1)}, bf16[512,4,64]{0,2,1:T(8,128)(2,1)}, u32[]{:S(2)}) copy-start(bf16[512,4,64]{0,2,1:T(8,128)(2,1)} %copy-done.1) | copy-start | bytes 786436
  427.1 491.6 %reduce-scatter.5.cloned.1.call-start = ((), (), s32[]{:S(2)}) async-start(), calls=%async_computation.13 | async-start | bytes 12976128 | tf_op jit(solution)/shard_map/reduce_scatter | solution.py:308
  460.9 88.2 %copy-start.22 = (f32[512,4,64]{0,2,1:T(8,128)S(1)}, f32[512,4,64]{0,2,1:T(8,128)}, u32[]{:S(2)}) copy-start(f32[512,4,64]{0,2,1:T(8,128)} %custom-call.4) | copy-start | bytes 1572868
  581.4 5.4 copy-start.28
  597.0 5.4 copy-start.28
  612.5 5.4 copy-start.28
  628.5 5.4 copy-start.28
  644.5 5.5 copy-start.28
  660.2 5.4 copy-start.28
  711.8 664.2 %reduce-scatter.9.cloned.1.call-start = ((), (), s32[]{:S(2)}) async-start(), calls=%async_computation.15 | async-start | bytes 22167552 | tf_op jit(solution)/shard_map/reduce_scatter | solution.py:311
  722.2 8.0 slice-start
  722.9 7.3 slice-start.1
  722.9 7.3 copy-start.7
  722.9 7.3 copy-start.41
  (50 other events, 123.4 us)
Sparse Core Ops, SparseCore 0:
  10.9 72.5 all-gather.7
  105.2 95.5 all-gather.17
  203.8 59.7 all-gather.9
  266.3 89.5 all-gather.11
  358.4 50.0 all-gather.13
  410.4 49.7 all-gather.15
  463.1 142.1 reduce-scatter.6
  611.8 145.7 reduce-scatter.10
  764.2 154.4 reduce-scatter.4
  921.5 454.4 reduce-scatter.8
